TPU v7x, 32 devices: a whole 2x2x4 slice. The times are simulated.
32 devices in a mesh: fsdp: 16 (over z, y, core), tp: 2 (over x).
Axes of the slice: x: 2, y: 2, z: 4, core: 2. Of those that a mesh axis runs over, the one named last changes fastest.
Arguments:
- tokens: bfloat16 [16, 1024, 1152], P('fsdp', 'tp'), may hold values from -6 to 6
- condition: bfloat16 [16, 1152], P('fsdp'), may hold values from -3 to 3
- mod_weight: bfloat16 [1152, 6912], P('tp', 'fsdp'), may hold values from -0.088388348 to 0.088388348
- mod_bias: bfloat16 [6912], P('fsdp'), may hold values from -1.5 to 1.5
- qkv_weight: bfloat16 [1152, 3, 1152], P('fsdp', None, 'tp'), may hold values from -0.088388348 to 0.088388348
- qv_bias: bfloat16 [2, 1152], P(None, 'fsdp'), may hold values from -2 to 2
- out_weight: bfloat16 [1152, 1152], P('tp', 'fsdp'), may hold values from -0.75 to 0.75
- out_bias: bfloat16 [1152], P('fsdp'), may hold values from -3 to 3
- up_weight: bfloat16 [1152, 4608], P('fsdp', 'tp'), may hold values from -0.1875 to 0.1875
- up_bias: bfloat16 [4608], P('fsdp'), may hold values from -3 to 3
- down_weight: bfloat16 [4608, 1152], P('tp', 'fsdp'), may hold values from -0.09375 to 0.09375
- down_bias: bfloat16 [1152], P('fsdp'), may hold values from -3 to 3
- cotangent: bfloat16 [16, 1024, 1152], P('fsdp', 'tp'), may hold values from -6 to 6
Outputs:
- result: bfloat16 [16, 1024, 1152], P('fsdp', 'tp')
- tokens_grad: bfloat16 [16, 1024, 1152], P('fsdp', 'tp')
- condition_grad: float32 [16, 1152], P('fsdp', 'tp')
- mod_weight_grad: float32 [1152, 6912], P('tp', 'fsdp')
- mod_bias_grad: float32 [6912], P('fsdp')
- qkv_weight_grad: float32 [1152, 3, 1152], P('fsdp', None, 'tp')
- qv_bias_grad: float32 [2, 1152], P(None, 'fsdp')
- out_weight_grad: float32 [1152, 1152], P('tp', 'fsdp')
- out_bias_grad: float32 [1152], P('fsdp')
- up_weight_grad: float32 [1152, 4608], P('fsdp', 'tp')
- up_bias_grad: float32 [4608], P('fsdp')
- down_weight_grad: float32 [4608, 1152], P('tp', 'fsdp')
- down_bias_grad: float32 [1152], P('fsdp')
All inputs are finite; a program needn't handle non-finite values.
Results may differ from a plain program's by a relative error of at most 0.015.
Values may be sent and summed in bfloat16 or wider, within the bound.
A program may use at most 256 MiB of HBM per device.

v0:
```python
import math
import jax
import jax.numpy as jnp
from jax import lax
from jax.sharding import PartitionSpec as P

HEAD_DIM = 72
EPSILON = 1e-06
HIGH = lax.Precision.HIGHEST


def normalize(values):
    center = values - jnp.mean(values, axis=-1, keepdims=True)
    variance = jnp.mean(center * center, axis=-1, keepdims=True)
    inverse = lax.rsqrt(variance + EPSILON)
    return (center * inverse, inverse)


def norm_back(grad_norm, normed, inverse):
    first_mean = jnp.mean(grad_norm, axis=-1, keepdims=True)
    second_mean = jnp.mean(grad_norm * normed, axis=-1, keepdims=True)
    return inverse * (grad_norm - first_mean - normed * second_mean)


def inner_rows(left, right):
    return lax.dot_general(
        left, right, (((0,), (0,)), ((), ())), preferred_element_type=jnp.float32
    )


def outer_cols(left, right):
    return lax.dot_general(
        left, right, (((1,), (1,)), ((), ())), preferred_element_type=jnp.float32
    )


def gelu_tanh(values):
    return jax.nn.gelu(values, approximate=True)


def to_heads(flat, head_count):
    return flat.reshape(flat.shape[0], head_count, HEAD_DIM).transpose(1, 0, 2)


def from_heads(stacked):
    return stacked.transpose(1, 0, 2).reshape(stacked.shape[1], stacked.shape[0] * HEAD_DIM)


def shards(
    tokens,
    condition,
    mod_weight,
    mod_bias,
    qkv_weight,
    qv_bias,
    out_weight,
    out_bias,
    up_weight,
    up_bias,
    down_weight,
    down_bias,
    cotangent,
):
    tp_count = lax.axis_size("tp")
    tp_place = lax.axis_index("tp")
    local_rows = tokens.shape[1]
    width = tokens.shape[2]
    seq_len = local_rows * tp_count
    share = width // tp_count
    (
        mod_full,
        mod_shift,
        qkv_full,
        qv_full,
        out_full,
        out_shift,
        up_full,
        up_shift,
        down_full,
        down_shift,
    ) = (
        lax.all_gather(mod_weight, "fsdp", axis=1, tiled=True),
        lax.all_gather(mod_bias, "fsdp", axis=0, tiled=True),
        lax.all_gather(qkv_weight, "fsdp", axis=0, tiled=True),
        lax.all_gather(qv_bias, "fsdp", axis=1, tiled=True),
        lax.all_gather(out_weight, "fsdp", axis=1, tiled=True),
        lax.all_gather(out_bias, "fsdp", axis=0, tiled=True),
        lax.all_gather(up_weight, "fsdp", axis=0, tiled=True),
        lax.all_gather(up_bias, "fsdp", axis=0, tiled=True),
        lax.all_gather(down_weight, "fsdp", axis=1, tiled=True),
        lax.all_gather(down_bias, "fsdp", axis=0, tiled=True),
    )
    head_cols = qkv_full.shape[2]
    head_count = head_cols // HEAD_DIM
    hidden_cols = up_full.shape[1]
    cond_row = condition[0].astype(jnp.float32)
    cond_part = lax.dynamic_slice_in_dim(cond_row, tp_place * share, share)
    silu_part, silu_pull = jax.vjp(jax.nn.silu, cond_part)
    silu_low = silu_part.astype(jnp.bfloat16)
    partial_mod = jnp.dot(silu_low[None, :], mod_full, preferred_element_type=jnp.float32)[0]
    modulation = lax.psum(partial_mod, "tp") + mod_shift.astype(jnp.float32)
    pieces = modulation.reshape(6, width)
    shift_one = pieces[0]
    scale_one = pieces[1]
    gate_one = pieces[2]
    shift_two = pieces[3]
    scale_two = pieces[4]
    gate_two = pieces[5]
    rows_in = tokens[0].astype(jnp.float32)
    normed_one, inverse_one = normalize(rows_in)
    hidden_one = lax.all_gather(
        (normed_one * (1.0 + scale_one) + shift_one).astype(jnp.bfloat16), "tp", axis=0, tiled=True
    )
    qkv_matrix = qkv_full.reshape(width, 3 * head_cols)
    projected = jnp.dot(hidden_one, qkv_matrix, preferred_element_type=jnp.float32).reshape(
        seq_len, 3, head_cols
    )
    qv_local = lax.dynamic_slice_in_dim(
        qv_full.astype(jnp.float32), tp_place * head_cols, head_cols, 1
    )
    queries = to_heads((projected[:, 0] + qv_local[0]).astype(jnp.bfloat16), head_count)
    keys_all = to_heads(projected[:, 1].astype(jnp.bfloat16), head_count)
    values_all = to_heads((projected[:, 2] + qv_local[1]).astype(jnp.bfloat16), head_count)
    block = min(512, seq_len)
    block_count = seq_len // block
    scaling = 1.0 / math.sqrt(HEAD_DIM)
    query_blocks = queries.reshape(head_count, block_count, block, HEAD_DIM).transpose(1, 0, 2, 3)

    def attend(query_block):
        scores = (
            jnp.einsum("hqd,hkd->hqk", query_block, keys_all, preferred_element_type=jnp.float32)
            * scaling
        )
        highest = jnp.max(scores, axis=-1, keepdims=True)
        raised = jnp.exp(scores - highest)
        totals = jnp.sum(raised, axis=-1, keepdims=True)
        weights = (raised / totals).astype(jnp.bfloat16)
        output = jnp.einsum("hqk,hkd->hqd", weights, values_all, preferred_element_type=jnp.float32)
        return (output, (highest + jnp.log(totals))[..., 0])

    attended_blocks, log_totals = lax.map(attend, query_blocks)
    attended = attended_blocks.transpose(1, 0, 2, 3).reshape(head_count, seq_len, HEAD_DIM)
    attended_low = from_heads(attended).astype(jnp.bfloat16)
    picked = attended_low
    branch_one = lax.psum_scatter(
        jnp.dot(picked, out_full, preferred_element_type=jnp.float32),
        "tp",
        scatter_dimension=0,
        tiled=True,
    ) + out_shift.astype(jnp.float32)
    middle = rows_in + gate_one * branch_one
    normed_two, inverse_two = normalize(middle)
    hidden_two = lax.all_gather(
        (normed_two * (1.0 + scale_two) + shift_two).astype(jnp.bfloat16), "tp", axis=0, tiled=True
    )
    up_local = lax.dynamic_slice_in_dim(
        up_shift.astype(jnp.float32), tp_place * hidden_cols, hidden_cols
    )
    before = jnp.dot(hidden_two, up_full, preferred_element_type=jnp.float32) + up_local
    activated, gelu_pull = jax.vjp(gelu_tanh, before)
    activated_low = activated.astype(jnp.bfloat16)
    picked = activated_low
    branch_two = lax.psum_scatter(
        jnp.dot(picked, down_full, preferred_element_type=jnp.float32).astype(jnp.bfloat16),
        "tp",
        scatter_dimension=0,
        tiled=True,
    ).astype(jnp.float32) + down_shift.astype(jnp.float32)
    outcome = (middle + gate_two * branch_two).astype(jnp.bfloat16)
    grad_rows = cotangent[0].astype(jnp.float32)
    grad_gate_two = jnp.sum(grad_rows * branch_two, axis=0)
    grad_branch_two = lax.all_gather(
        (grad_rows * gate_two).astype(jnp.bfloat16), "tp", axis=0, tiled=True
    )
    down_bias_term = jnp.sum(grad_branch_two.astype(jnp.float32), axis=0)
    down_weight_term = inner_rows(activated_low, grad_branch_two)
    grad_before = gelu_pull(outer_cols(grad_branch_two, down_full))[0].astype(jnp.bfloat16)
    up_bias_part = jnp.sum(grad_before.astype(jnp.float32), axis=0)
    up_weight_term = inner_rows(hidden_two, grad_before)
    picked = grad_before
    grad_hidden_two = lax.psum_scatter(
        outer_cols(picked, up_full), "tp", scatter_dimension=0, tiled=True
    )
    grad_scale_two = jnp.sum(grad_hidden_two * normed_two, axis=0)
    grad_shift_two = jnp.sum(grad_hidden_two, axis=0)
    grad_middle = grad_rows + norm_back(
        grad_hidden_two * (1.0 + scale_two), normed_two, inverse_two
    )
    grad_gate_one = jnp.sum(grad_middle * branch_one, axis=0)
    grad_branch_one = lax.all_gather(
        (grad_middle * gate_one).astype(jnp.bfloat16), "tp", axis=0, tiled=True
    )
    out_bias_term = jnp.sum(grad_branch_one.astype(jnp.float32), axis=0)
    out_weight_term = inner_rows(attended_low, grad_branch_one)
    grad_attended = outer_cols(grad_branch_one, out_full).astype(jnp.bfloat16)
    grad_blocks = (
        to_heads(grad_attended, head_count)
        .reshape(head_count, block_count, block, HEAD_DIM)
        .transpose(1, 0, 2, 3)
    )

    def attend_back(carry, inputs):
        grad_keys, grad_values = carry
        query_block, log_block, grad_block = inputs
        scores = (
            jnp.einsum("hqd,hkd->hqk", query_block, keys_all, preferred_element_type=jnp.float32)
            * scaling
        )
        weights = jnp.exp(scores - log_block[..., None])
        grad_weights = jnp.einsum(
            "hqd,hkd->hqk", grad_block, values_all, preferred_element_type=jnp.float32
        )
        centered = jnp.sum(weights * grad_weights, axis=-1, keepdims=True)
        grad_scores = (weights * (grad_weights - centered)).astype(jnp.bfloat16)
        grad_query = (
            jnp.einsum("hqk,hkd->hqd", grad_scores, keys_all, preferred_element_type=jnp.float32)
            * scaling
        )
        grad_keys = (
            grad_keys
            + jnp.einsum(
                "hqk,hqd->hkd", grad_scores, query_block, preferred_element_type=jnp.float32
            )
            * scaling
        )
        grad_values = grad_values + jnp.einsum(
            "hqk,hqd->hkd",
            weights.astype(jnp.bfloat16),
            grad_block,
            preferred_element_type=jnp.float32,
        )
        return ((grad_keys, grad_values), grad_query)

    zero_heads = jnp.zeros((head_count, seq_len, HEAD_DIM), jnp.float32)
    (grad_keys, grad_values), grad_query_blocks = lax.scan(
        attend_back, (zero_heads, zero_heads), (query_blocks, log_totals, grad_blocks)
    )
    grad_queries = grad_query_blocks.transpose(1, 0, 2, 3).reshape(head_count, seq_len, HEAD_DIM)
    grad_projected = jnp.stack(
        [from_heads(grad_queries), from_heads(grad_keys), from_heads(grad_values)], axis=1
    ).astype(jnp.bfloat16)
    qv_bias_part = jnp.sum(grad_projected[:, 0::2].astype(jnp.float32), axis=0)
    grad_flat = grad_projected.reshape(seq_len, 3 * head_cols)
    qkv_weight_term = inner_rows(hidden_one, grad_flat).reshape(width, 3, head_cols)
    picked = grad_flat
    grad_hidden_one = lax.psum_scatter(
        outer_cols(picked, qkv_matrix).astype(jnp.bfloat16), "tp", scatter_dimension=0, tiled=True
    ).astype(jnp.float32)
    grad_scale_one = jnp.sum(grad_hidden_one * normed_one, axis=0)
    grad_shift_one = jnp.sum(grad_hidden_one, axis=0)
    grad_tokens = grad_middle + norm_back(
        grad_hidden_one * (1.0 + scale_one), normed_one, inverse_one
    )
    grad_mod_part = jnp.concatenate(
        [
            grad_shift_one,
            grad_scale_one,
            grad_gate_one,
            grad_shift_two,
            grad_scale_two,
            grad_gate_two,
        ]
    )
    qv_padded = lax.dynamic_update_slice_in_dim(
        jnp.zeros((2, width), jnp.float32), qv_bias_part, tp_place * head_cols, 1
    )
    up_padded = lax.dynamic_update_slice_in_dim(
        jnp.zeros((up_shift.shape[0],), jnp.float32), up_bias_part, tp_place * hidden_cols, 0
    )
    grad_mod, qv_bias_term, up_bias_term = (
        lax.psum(grad_mod_part.astype(jnp.bfloat16), "tp").astype(jnp.float32),
        lax.psum(qv_padded.astype(jnp.bfloat16), "tp").astype(jnp.float32),
        lax.psum(up_padded.astype(jnp.bfloat16), "tp").astype(jnp.float32),
    )
    grad_silu = jnp.dot(mod_full.astype(jnp.float32), grad_mod, precision=HIGH)
    cond_grad = silu_pull(grad_silu)[0][None, :]
    mod_weight_term = silu_low.astype(jnp.float32)[:, None] * grad_mod[None, :]
    (
        mod_weight_grad,
        mod_bias_grad,
        qkv_weight_grad,
        qv_bias_grad,
        out_weight_grad,
        out_bias_grad,
        up_weight_grad,
        up_bias_grad,
        down_weight_grad,
        down_bias_grad,
    ) = (
        lax.psum_scatter(mod_weight_term, "fsdp", scatter_dimension=1, tiled=True),
        lax.psum_scatter(grad_mod, "fsdp", scatter_dimension=0, tiled=True),
        lax.psum_scatter(qkv_weight_term, "fsdp", scatter_dimension=0, tiled=True),
        lax.psum_scatter(qv_bias_term, "fsdp", scatter_dimension=1, tiled=True),
        lax.psum_scatter(out_weight_term, "fsdp", scatter_dimension=1, tiled=True),
        lax.psum_scatter(out_bias_term, "fsdp", scatter_dimension=0, tiled=True),
        lax.psum_scatter(up_weight_term, "fsdp", scatter_dimension=0, tiled=True),
        lax.psum_scatter(up_bias_term, "fsdp", scatter_dimension=0, tiled=True),
        lax.psum_scatter(down_weight_term, "fsdp", scatter_dimension=1, tiled=True),
        lax.psum_scatter(down_bias_term, "fsdp", scatter_dimension=0, tiled=True),
    )
    return (
        outcome[None],
        grad_tokens.astype(jnp.bfloat16)[None],
        cond_grad,
        mod_weight_grad,
        mod_bias_grad,
        qkv_weight_grad,
        qv_bias_grad,
        out_weight_grad,
        out_bias_grad,
        up_weight_grad,
        up_bias_grad,
        down_weight_grad,
        down_bias_grad,
    )


def solution(mesh):
    return jax.shard_map(
        shards,
        mesh=mesh,
        in_specs=(
            P("fsdp", "tp", None),
            P("fsdp", None),
            P("tp", "fsdp"),
            P("fsdp"),
            P("fsdp", None, "tp"),
            P(None, "fsdp"),
            P("tp", "fsdp"),
            P("fsdp"),
            P("fsdp", "tp"),
            P("fsdp"),
            P("tp", "fsdp"),
            P("fsdp"),
            P("fsdp", "tp", None),
        ),
        out_specs=(
            P("fsdp", "tp", None),
            P("fsdp", "tp", None),
            P("fsdp", "tp"),
            P("tp", "fsdp"),
            P("fsdp"),
            P("fsdp", None, "tp"),
            P(None, "fsdp"),
            P("tp", "fsdp"),
            P("fsdp"),
            P("fsdp", "tp"),
            P("fsdp"),
            P("tp", "fsdp"),
            P("fsdp"),
        ),
        check_vma=False,
    )
```

profile of v0, /device:TPU:0, one launch (start us, length us, event | category | flops | bytes accessed | tf_op | source)
XLA Modules:
  0.0 1452.1 jit_solution(4694295346993704896)
XLA Ops:
  17.4 65.6 %all-reduce.11 = (bf16[6912]{0:T(1024)(128)(2,1)S(1)}, bf16[1152]{0:T(1024)(128)(2,1)}, bf16[4608]{0:T(1024)(128)(2,1)}, bf16[1152]{0:T(1024)(128)(2,1)}) all-reduce(bf16[6912]{0:T(1024)(128)(2,1)S(1)} %dynamic-update-slice, bf16[1152]{0:T(1024)(128)(2,1)S(1)} %dynamic-update-slice.1, ...), channel_id=1, replica_groups=mesh['fsdp'=16,'tp'=2] {'fsdp'}, use_global_device_ids=true, to_apply=%add | all-reduce | flops 13824 | bytes 55296
  85.0 6.6 all-gather.11.cloned.1.call-done
  91.6 5.9 convolution_reduce_fusion
  97.5 8.3 psum.28
  109.2 18.8 %all-gather = bf16[16,72,2]{1,2,0:T(2,128)(2,1)S(1)} all-gather(bf16[1,72,2]{1,2,0:T(2,128)(2,1)S(1)} %bitcast.228), channel_id=1, replica_groups=mesh['fsdp'=16,'tp'=2] {'fsdp'}, dimensions={0}, use_global_device_ids=true | all-gather | bytes 4896 | tf_op jit(solution)/shard_map/all_gather | solution.py:85
  128.4 15.3 %all-gather.15.cloned.1.call-done = bf16[1152,3,576]{2,0,1:T(8,128)(2,1)} async-done(((bf16[72,3,576]{2,0,1:T(8,128)(2,1)}), bf16[1152,3,576]{2,0,1:T(8,128)(2,1)}) %all-gather.15.cloned.1.call-update) | async-done | bytes 3981328 | tf_op jit(solution)/shard_map/all_gather | solution.py:84
  143.7 6.5 copy.43
  150.2 30.2 %all-gather.13.cloned.1.call-done = bf16[1024,1152]{1,0:T(8,128)(2,1)} async-done(((bf16[512,1152]{1,0:T(8,128)(2,1)}), bf16[1024,1152]{1,0:T(8,128)(2,1)}) %all-gather.13.cloned.1.call-update) | async-done | bytes 2359312 | tf_op jit(solution)/shard_map/all_gather | solution.py:111
  180.4 7.3 fusion.40
  194.1 24.2 %while.27 = (s32[]{:T(128)}, bf16[2,8,512,72]{2,3,1,0:T(8,128)(2,1)}, f32[2,8,512]{2,1,0:T(8,128)}, bf16[2,8,512,72]{2,3,1,0:T(8,128)(2,1)S(1)}, bf16[8,1024,72]...) while((s32[]{:T(128)}, bf16[2,8,512,72]{2,3,1,0:T(8,128)(2,1)}, ...), condition=%wide.region_6.7_spmd, body=%wide.region_3.6_spmd.sunk | while | flops 1245704192 | bytes 64291024 | solution.py:141
  194.1 2.5 multiply_reduce_fusion.9
  196.6 3.5 fusion.132
  200.2 4.4 fusion.133
  206.2 2.5 multiply_reduce_fusion.9
  208.7 3.5 fusion.132
  212.2 4.4 fusion.133
  218.2 2.5 copy.55
  221.8 6.1 fusion.81
  229.3 57.8 %reduce-scatter.13.cloned.1.call-done = f32[512,1152]{1,0:T(8,128)} async-done(((f32[1024,1152]{1,0:T(8,128)}), f32[512,1152]{1,0:T(8,128)}) %reduce-scatter.13.cloned.1.call-update) | async-done | bytes 2359312 | tf_op jit(solution)/shard_map/reduce_scatter | solution.py:145
  293.3 2.5 fusion.62
  297.4 48.3 %all-gather.21.cloned.1.call-done = bf16[1152,2304]{1,0:T(8,128)(2,1)} async-done(((bf16[72,2304]{1,0:T(8,128)(2,1)}), bf16[1152,2304]{1,0:T(8,128)(2,1)}) %all-gather.21.cloned.1.call-update) | async-done | bytes 5308432 | tf_op jit(solution)/shard_map/all_gather | solution.py:88
  345.7 36.9 %all-gather.19.cloned.1.call-done = bf16[1024,1152]{1,0:T(8,128)(2,1)} async-done(((bf16[512,1152]{1,0:T(8,128)(2,1)}), bf16[1024,1152]{1,0:T(8,128)(2,1)}) %all-gather.19.cloned.1.call-update) | async-done | bytes 2359312 | tf_op jit(solution)/shard_map/all_gather | solution.py:153
  382.6 11.4 fusion.82
  394.0 47.4 %all-gather.23.cloned.1.call-done = bf16[2304,1152]{0,1:T(8,128)(2,1)} async-done(((bf16[2304,72]{0,1:T(8,128)(2,1)}), bf16[2304,1152]{0,1:T(8,128)(2,1)}) %all-gather.23.cloned.1.call-update) | async-done | bytes 5308432 | tf_op jit(solution)/shard_map/all_gather | solution.py:90
  441.4 36.9 %all-gather.25.cloned.1.call-done = bf16[1024,1152]{1,0:T(8,128)(2,1)} async-done(((bf16[512,1152]{1,0:T(8,128)(2,1)}), bf16[1024,1152]{1,0:T(8,128)(2,1)}) %all-gather.25.cloned.1.call-update) | async-done | bytes 2359312 | tf_op jit(solution)/shard_map/all_gather | solution.py:172
  478.2 15.4 %convert_reduce_fusion = (bf16[2304]{0:T(1024)(128)(2,1)}, bf16[1024,2304]{1,0:T(8,128)(2,1)S(1)}) fusion(f32[1024,2304]{1,0:T(8,128)} %fusion.82, f32[2304]{0:T(1024)} %dynamic-slice_convert_fusion, bf16[1024,1152]{1,0:T(8,128)(2,1)} %all-gather.25.cloned.1.call-done, bf16[2304,1152]{0,1:T(8,128)(2,1)} %all-gather.23.cloned.1.call-done), kind=kOutput, calls=%fused_computation.50 | convolution fusion | flops 5490079744 | bytes 21837312 | tf_op jit(solution)/shard_map/dot_general | solution.py:32
  495.7 10.4 fusion.83
  506.6 13.4 convolution_convert_fusion
  521.4 44.8 %reduce-scatter.17.cloned.1.call-done = f32[512,1152]{1,0:T(8,128)} async-done(((f32[1024,1152]{1,0:T(8,128)}), f32[512,1152]{1,0:T(8,128)}) %reduce-scatter.17.cloned.1.call-update) | async-done | bytes 2359312 | tf_op jit(solution)/shard_map/reduce_scatter | solution.py:181
  566.3 3.9 multiply_reduce_fusion.2
  570.8 32.5 %reduce-scatter.15.cloned.1.call-done = bf16[512,1152]{1,0:T(8,128)(2,1)} async-done(((bf16[1024,1152]{1,0:T(8,128)(2,1)}), bf16[512,1152]{1,0:T(8,128)(2,1)}) %reduce-scatter.15.cloned.1.call-update) | async-done | bytes 1179664 | tf_op jit(solution)/shard_map/reduce_scatter | solution.py:163
  603.3 6.2 multiply_reduce_fusion.3
  612.1 36.2 %all-gather.27.cloned.1.call-done = bf16[1024,1152]{1,0:T(8,128)(2,1)} async-done(((bf16[512,1152]{1,0:T(8,128)(2,1)}), bf16[1024,1152]{1,0:T(8,128)(2,1)}) %all-gather.27.cloned.1.call-update) | async-done | bytes 2359312 | tf_op jit(solution)/shard_map/all_gather | solution.py:190
  648.2 4.8 convolution_convert_fusion.1
  653.1 4.0 reshape.171
  657.1 2.5 copy.48
  660.7 116.9 %while.28 = (s32[]{:T(128)}, f32[8,1024,72]{1,2,0:T(8,128)}, f32[8,1024,72]{1,2,0:T(8,128)}, bf16[2,8,512,72]{2,3,1,0:T(8,128)(2,1)}, bf16[2,8,512,72]{2,3,1,0:T...) while((s32[]{:T(128)}, f32[8,1024,72]{1,2,0:T(8,128)}, ...), condition=%wide.region_16.17_spmd.clone, body=%wide.region_14.16_spmd.clone.sunk | while | flops 3073470464 | bytes 271434112 | solution.py:235
  661.6 8.1 fusion.143
  669.8 10.3 select_add_fusion.5
  680.1 14.5 multiply_reduce_fusion.10
  697.0 10.5 multiply_convert_fusion.8
  707.5 7.3 fusion.144
  714.8 3.1 select_add_fusion.4
  718.7 8.1 fusion.143
  726.9 11.1 select_add_fusion.5
  738.0 14.5 multiply_reduce_fusion.10
  754.8 10.5 multiply_convert_fusion.8
  765.3 7.3 fusion.144
  772.7 4.9 select_add_fusion.4
  782.1 7.2 bitcast_convert_fusion
  789.3 5.7 fusion.84
  795.8 12.4 fusion.73
  808.3 11.5 fusion.85
  820.1 9.5 fusion.42
  834.6 2.9 fusion.61
  838.8 8.4 all-reduce.12
  847.2 7.3 broadcast_multiply_fusion
  859.3 4.9 convolution_reduce_fusion.1
  864.9 61.7 %all-reduce.10 = (f32[6912]{0:T(1024)}, f32[2,1152]{1,0:T(2,128)}, f32[1152]{0:T(1024)}, f32[4608]{0:T(1024)}, f32[1152]{0:T(1024)}) all-reduce(bf16[6912]{0:T(1024)(128)(2,1)} %copy-done.25, bf16[2,1152]{1,0:T(2,128)(2,1)} %get-tuple-element.224, f32[1152]{0:T(1024)} %convert_reduce_fusion.2, ...), channel_id=7, replica_groups=mesh['fsdp'=16,'tp'=2] {'fsdp'}, use_global_device_ids=true, to_apply=%region_28.29.clone | all-reduce | flops 16128 | bytes 101376
  934.5 3.2 fusion.69
  937.6 80.0 %reduce-scatter.27.cloned.1.call-done = f32[2304,72]{0,1:T(8,128)} async-done(((f32[2304,1152]{0,1:T(8,128)}), f32[2304,72]{0,1:T(8,128)}) %reduce-scatter.27.cloned.1.call-update) | async-done | bytes 663568 | tf_op jit(solution)/shard_map/reduce_scatter | solution.py:298
  1017.6 124.5 %reduce-scatter.25.cloned.1.call-done = f32[72,2304]{1,0:T(8,128)} async-done(((f32[1152,2304]{1,0:T(8,128)}), f32[72,2304]{1,0:T(8,128)}) %reduce-scatter.25.cloned.1.call-update) | async-done | bytes 663568 | tf_op jit(solution)/shard_map/reduce_scatter | solution.py:296
  1142.1 111.3 %reduce-scatter.23.cloned.1.call-done = f32[72,3,576]{2,0,1:T(8,128)} async-done(((f32[1152,3,576]{2,0,1:T(8,128)}), f32[72,3,576]{2,0,1:T(8,128)}) %reduce-scatter.23.cloned.1.call-update) | async-done | bytes 497680 | tf_op jit(solution)/shard_map/reduce_scatter | solution.py:292
  1253.5 191.4 %reduce-scatter.21.cloned.1.call-done = f32[576,432]{0,1:T(8,128)} async-done(((f32[576,6912]{0,1:T(8,128)}), f32[576,432]{0,1:T(8,128)}) %reduce-scatter.21.cloned.1.call-update) | async-done | bytes 995344 | tf_op jit(solution)/shard_map/reduce_scatter | solution.py:290
  (240 shorter events, 71.1 us)
Async XLA Ops:
  7.2 77.3 %copy-start.10 = (bf16[1,512,1152]{2,1,0:T(8,128)(2,1)S(1)}, bf16[1,512,1152]{2,1,0:T(8,128)(2,1)}, u32[]{:S(2)}) copy-start(bf16[1,512,1152]{2,1,0:T(8,128)(2,1)} %param.17) | copy-start | bytes 3538948
  7.2 84.4 %all-gather.11.cloned.1.call-start = ((), (), s32[]{:S(2)}) async-start(), calls=%async_computation.9 | async-start | bytes 9400320 | tf_op jit(solution)/shard_map/all_gather | solution.py:82
  7.9 135.8 %all-gather.15.cloned.1.call-start = ((), (), s32[]{:S(2)}) async-start(), calls=%async_computation.11 | async-start | bytes 4700160 | tf_op jit(solution)/shard_map/all_gather | solution.py:84
  8.7 171.8 %all-gather.13.cloned.1.call-start = ((), (), s32[]{:S(2)}) async-start(), calls=%async_computation.10 | async-start | bytes 3538944 | tf_op jit(solution)/shard_map/all_gather | solution.py:111
  84.5 21.9 %copy-start.29 = (f32[512]{0:T(512)}, f32[512]{0:T(512)S(1)}, u32[]{:S(2)}) copy-start(f32[512]{0:T(512)S(1)} %broadcast_multiply_fusion.6) | copy-start | bytes 6148
  85.0 21.5 %copy-start.34 = (f32[512]{0:T(512)}, f32[512]{0:T(512)S(1)}, u32[]{:S(2)}) copy-start(f32[512]{0:T(512)S(1)} %add_rsqrt_fusion.1) | copy-start | bytes 6148
  97.5 11.7 copy-start.45
  108.6 113.2 %all-gather.17.cloned.1.call-start = ((), (), s32[]{:S(2)}) async-start(), calls=%async_computation.12 | async-start | bytes 1566720 | tf_op jit(solution)/shard_map/all_gather | solution.py:86
  109.2 177.9 %reduce-scatter.13.cloned.1.call-start = ((), (), s32[]{:S(2)}) async-start(), calls=%async_computation.13 | async-start | bytes 7077888 | tf_op jit(solution)/shard_map/reduce_scatter | solution.py:145
  196.6 3.6 copy-start.16
  200.1 4.4 copy-start.20
  208.7 3.6 copy-start.16
  212.2 4.4 copy-start.20
  227.9 59.2 %copy-start.27 = (f32[1152]{0:T(1024)S(1)}, f32[1152]{0:T(1024)}, u32[]{:S(2)}) copy-start(f32[1152]{0:T(1024)} %get-tuple-element.247) | copy-start | bytes 13828
  227.9 117.8 %all-gather.21.cloned.1.call-start = ((), (), s32[]{:S(2)}) async-start(), calls=%async_computation.15 | async-start | bytes 5640192 | tf_op jit(solution)/shard_map/all_gather | solution.py:88
  228.5 154.1 %all-gather.19.cloned.1.call-start = ((), (), s32[]{:S(2)}) async-start(), calls=%async_computation.14 | async-start | bytes 3538944 | tf_op jit(solution)/shard_map/all_gather | solution.py:153
  229.3 57.8 %copy-start.28 = (f32[1152]{0:T(1024)}, f32[1152]{0:T(1024)S(1)}, u32[]{:S(2)}) copy-start(f32[1152]{0:T(1024)S(1)} %convert_element_type.164) | copy-start | bytes 13828
  292.5 148.9 %all-gather.23.cloned.1.call-start = ((), (), s32[]{:S(2)}) async-start(), calls=%async_computation.16 | async-start | bytes 5640192 | tf_op jit(solution)/shard_map/all_gather | solution.py:90
  293.2 185.0 %all-gather.25.cloned.1.call-start = ((), (), s32[]{:S(2)}) async-start(), calls=%async_computation.18 | async-start | bytes 3538944 | tf_op jit(solution)/shard_map/all_gather | solution.py:172
  295.8 270.5 %reduce-scatter.17.cloned.1.call-start = ((), (), s32[]{:S(2)}) async-start(), calls=%async_computation.19 | async-start | bytes 7077888 | tf_op jit(solution)/shard_map/reduce_scatter | solution.py:181
  493.6 2.1 copy-start.46
  506.1 97.2 %reduce-scatter.15.cloned.1.call-start = ((), (), s32[]{:S(2)}) async-start(), calls=%async_computation.17 | async-start | bytes 3538944 | tf_op jit(solution)/shard_map/reduce_scatter | solution.py:163
  520.1 128.1 %all-gather.27.cloned.1.call-start = ((), (), s32[]{:S(2)}) async-start(), calls=%async_computation.20 | async-start | bytes 3538944 | tf_op jit(solution)/shard_map/all_gather | solution.py:190
  612.0 220.7 %reduce-scatter.19.cloned.1.call-start = ((), (), s32[]{:S(2)}) async-start(), calls=%async_computation.21 | async-start | bytes 3538944 | tf_op jit(solution)/shard_map/reduce_scatter | solution.py:246
  660.8 8.9 copy-start.2
  660.9 8.9 copy-start.4
  660.9 8.9 copy-start.8
  680.1 16.9 %copy-start = (f32[8,512,1024]{2,1,0:T(8,128)S(1)}, f32[8,512,1024]{2,1,0:T(8,128)}, u32[]{:S(2)}) copy-start(f32[8,512,1024]{2,1,0:T(8,128)} %fusion.143) | copy-start | bytes 50331652 | tf_op jit(solution)/shard_map/while
  707.5 7.3 copy-start.1
  707.5 7.3 copy-start.5
  714.8 3.1 copy-start.3
  714.8 3.1 copy-start.9
  717.9 8.9 copy-start.2
  717.9 8.9 copy-start.4
  717.9 8.9 copy-start.8
  738.0 16.9 %copy-start = (f32[8,512,1024]{2,1,0:T(8,128)S(1)}, f32[8,512,1024]{2,1,0:T(8,128)}, u32[]{:S(2)}) copy-start(f32[8,512,1024]{2,1,0:T(8,128)} %fusion.143) | copy-start | bytes 50331652 | tf_op jit(solution)/shard_map/while
  765.3 7.3 copy-start.1
  765.3 7.3 copy-start.5
  772.6 5.0 copy-start.3
  772.6 5.0 copy-start.9
  777.6 2.0 copy-start.6
  777.6 4.5 slice-start
  779.6 2.4 slice-start.1
  782.1 38.0 %copy-start.14 = (bf16[1024,3,576]{0,2,1:T(8,128)(2,1)}, bf16[1024,3,576]{0,2,1:T(8,128)(2,1)S(1)}, u32[]{:S(2)}) copy-start(bf16[1024,3,576]{0,2,1:T(8,128)(2,1)S(1)} %maximum_convert_fusion) | copy-start | bytes 10616836
  789.3 148.3 %reduce-scatter.29.cloned.1.call-start = ((), (), s32[]{:S(2)}) async-start(), calls=%async_computation.26 | async-start | bytes 3133440
  795.1 222.5 %reduce-scatter.27.cloned.1.call-start = ((), (), s32[]{:S(2)}) async-start(), calls=%async_computation.25 | async-start | bytes 11280384 | tf_op jit(solution)/shard_map/reduce_scatter | solution.py:298
  808.2 333.9 %reduce-scatter.25.cloned.1.call-start = ((), (), s32[]{:S(2)}) async-start(), calls=%async_computation.24 | async-start | bytes 11280384 | tf_op jit(solution)/shard_map/reduce_scatter | solution.py:296
  819.8 433.7 %reduce-scatter.23.cloned.1.call-start = ((), (), s32[]{:S(2)}) async-start(), calls=%async_computation.23 | async-start | bytes 9400320 | tf_op jit(solution)/shard_map/reduce_scatter | solution.py:292
  829.6 5.0 copy-start.11
  829.6 5.0 copy-start.23
  829.6 5.0 copy-start.30
  829.6 5.0 copy-start.35
  829.6 615.2 %reduce-scatter.21.cloned.1.call-start = ((), (), s32[]{:S(2)}) async-start(), calls=%async_computation.22 | async-start | bytes 18800640 | tf_op jit(solution)/shard_map/reduce_scatter | solution.py:290
  832.5 5.3 copy-start.39
  832.5 5.5 copy-start.41
  832.5 5.8 copy-start.40
  832.5 6.1 copy-start.38
  832.5 14.7 %copy-start.42 = (f32[576]{0:T(1024)S(1)}, f32[576]{0:T(1024)}, u32[]{:S(2)}) copy-start(f32[576]{0:T(1024)} %get-tuple-element.226) | copy-start | bytes 6916
  847.2 7.3 copy-start.25
  854.5 2.1 copy-start.18
  856.6 1.7 copy-start.19
  856.6 2.7 copy-start.26
  859.3 5.0 copy-start.33
  859.3 75.1 %copy-start.13 = (f32[512,1152]{1,0:T(8,128)S(1)}, f32[512,1152]{1,0:T(8,128)}, u32[]{:S(2)}) copy-start(f32[512,1152]{1,0:T(8,128)} %copy-done.12) | copy-start | bytes 7077892
  (15 other events, 15.5 us)
Sparse Core Ops, SparseCore 0:
  10.2 81.3 all-gather.10
  93.8 49.8 all-gather.14
  145.8 34.5 all-gather.12
  182.4 39.3 all-gather.16
  228.1 58.9 reduce-scatter.12
  289.3 56.3 all-gather.20
  347.9 34.6 all-gather.18
  385.0 56.3 all-gather.22
  443.6 34.6 all-gather.24
  506.2 59.9 reduce-scatter.16
  568.5 34.7 reduce-scatter.14
  612.1 36.0 all-gather.26
  789.4 34.6 reduce-scatter.18
  828.5 65.4 reduce-scatter.28
  898.5 119.1 reduce-scatter.26
  1022.1 119.9 reduce-scatter.24
  1146.7 106.7 reduce-scatter.22
  1258.7 186.1 reduce-scatter.20
where the time goes:
time: 1460 us; the launch traced here: 1450 us
  waiting for transfers between devices  904 us (62%)
  matrix products  229 us (16%)
  blocking collectives  163 us (11%)
  other arithmetic  78.6 us (5%)
  local copies, waits for them, and re-layouts  56 us (4%)
  between operations  19.3 us (1%)
    reduce_scatter x1, waiting for transfers between devices, shards(): lax.psum_scatter(mod_weight_term, 'fsdp', scatter_dimension=1, tiled=True)  191 us
    unnamed x2, blocking collectives  127 us
    reduce_scatter x1, waiting for transfers between devices, shards(): lax.psum_scatter(up_weight_term, 'fsdp', scatter_dimension=0, tiled=True)  124 us
    reduce_scatter x1, waiting for transfers between devices, shards(): lax.psum_scatter(qkv_weight_term, 'fsdp', scatter_dimension=0, tiled=True)  111 us
    reduce_scatter x1, waiting for transfers between devices, shards(): lax.psum_scatter(down_weight_term, 'fsdp', scatter_dimension=1, tiled=True)  80 us
    reduce_scatter x1, waiting for transfers between devices, shards(): lax.psum_scatter(jnp.dot(picked, out_full, preferred_element_type=jnp.flo...  57.8 us
    all_gather x1, waiting for transfers between devices, shards(): lax.all_gather(up_weight, 'fsdp', axis=0, tiled=True)  48.3 us
    all_gather x1, waiting for transfers between devices, shards(): lax.all_gather(down_weight, 'fsdp', axis=1, tiled=True)  47.4 us
  transfers between devices with their start and end apart: 18, of which 16 were waited for; matrix products, arithmetic and copies ran while one was open for 12% of the time, Pallas kernels for 0%

commit v1 on v0

--- a/solution.py
+++ b/solution.py
@@ -1,12 +1,47 @@
+import functools
 import math
 import jax
 import jax.numpy as jnp
 from jax import lax
 from jax.sharding import PartitionSpec as P
+from jax.lax import axis_index, axis_size, ppermute
 
 HEAD_DIM = 72
 EPSILON = 1e-06
 HIGH = lax.Precision.HIGHEST
+
+
+def arrange_the_yards(mine_x, dim_at):
+    mine_x = jnp.moveaxis(mine_x, 0, dim_at)
+    piece_next = mine_x.shape
+    found_now = mine_x.reshape(
+        *piece_next[:dim_at], piece_next[dim_at] * piece_next[dim_at + 1], *piece_next[dim_at + 2 :]
+    )
+    return found_now
+
+
+def group_put(inp, axis_name, out_dim):
+    n_parts = axis_size(axis_name)
+    inbox = []
+    for j0 in range(n_parts):
+        inbox.append((j0, (j0 + 1) % n_parts))
+    history = []
+    for i, m in inbox:
+        history.append((m, i))
+    response, prior = ([], [])
+    for at in range(n_parts - 1):
+        if at % 2 == 0:
+            response.append(ppermute(response[-1] if response else inp, axis_name, inbox))
+        else:
+            prior.append(ppermute(prior[-1] if prior else inp, axis_name, history))
+    main = jnp.stack([*response[::-1], inp, *prior])
+    formed = axis_index(axis_name) - len(response)
+    main = main[(jnp.arange(n_parts) - formed) % n_parts]
+    t1 = arrange_the_yards(main, out_dim)
+    return t1
+
+
+serve_forms = functools.partial(group_put, axis_name="fsdp", out_dim=1)
 
 
 def normalize(values):
@@ -87,7 +122,7 @@
         lax.all_gather(out_bias, "fsdp", axis=0, tiled=True),
         lax.all_gather(up_weight, "fsdp", axis=0, tiled=True),
         lax.all_gather(up_bias, "fsdp", axis=0, tiled=True),
-        lax.all_gather(down_weight, "fsdp", axis=1, tiled=True),
+        serve_forms(down_weight),
         lax.all_gather(down_bias, "fsdp", axis=0, tiled=True),
     )
     head_cols = qkv_full.shape[2]

time: 1460 us -> 1400 us (0.959)
  waiting for transfers between devices: 904 us -> 790 us
  starting transfers between devices: 1.7 us -> 33.9 us
  local copies, waits for them, and re-layouts: 56 us -> 83.7 us
    reduce_scatter x1, waiting for transfers between devices: 57.8 us -> 0.01 us  [shards(): lax.psum_scatter(jnp.dot(picked, out_full, preferred_element_type=jnp.flo...]
    all_gather x1 -> x0, waiting for transfers between devices: 47.4 us -> none  [shards(): lax.all_gather(down_weight, 'fsdp', axis=1, tiled=True)]
    ppermute x0 -> x15, waiting for transfers between devices: none -> 41.9 us  [the longest x8 40.4 us: group_put(): ppermute(response[-1] if response else inp, axis_name, inbox)]
    all_gather x1, waiting for transfers between devices: 48.3 us -> 7.82 us  [shards(): lax.all_gather(up_weight, 'fsdp', axis=0, tiled=True)]
    ppermute x0 -> x15, starting transfers between devices: none -> 32.8 us  [the longest x7 32.5 us: group_put(): prior.append(ppermute(prior[-1] if prior else inp, axis_name, history))]
    unnamed x94 -> x145, local copies, waits for them, and re-layouts: 24.7 us -> 44.7 us
  transfers between devices with their start and end apart: 18 -> 32, of which waited for: 16 -> 24; matrix products, arithmetic and copies ran while one was open for 12% -> 14% of each run, Pallas kernels for 0% -> 0%
where the time goes in v1:
time: 1400 us; the launch traced here: 1390 us
  waiting for transfers between devices  790 us (56%)
  matrix products  227 us (16%)
  blocking collectives  163 us (12%)
  local copies, waits for them, and re-layouts  83.7 us (6%)
  other arithmetic  78.1 us (6%)
  starting transfers between devices  33.9 us (2%)
  between operations  18.9 us (1%)
    reduce_scatter x1, waiting for transfers between devices, shards(): lax.psum_scatter(mod_weight_term, 'fsdp', scatter_dimension=1, tiled=True)  191 us
    unnamed x2, blocking collectives  127 us
    reduce_scatter x1, waiting for transfers between devices, shards(): lax.psum_scatter(up_weight_term, 'fsdp', scatter_dimension=0, tiled=True)  124 us
    reduce_scatter x1, waiting for transfers between devices, shards(): lax.psum_scatter(qkv_weight_term, 'fsdp', scatter_dimension=0, tiled=True)  111 us
    reduce_scatter x1, waiting for transfers between devices, shards(): lax.psum_scatter(down_weight_term, 'fsdp', scatter_dimension=1, tiled=True)  80.3 us
    reduce_scatter x1, waiting for transfers between devices, shards(): lax.psum_scatter(outer_cols(picked, up_full), 'tp', scatter_dimension=0,...  45.1 us
    unnamed x145, local copies, waits for them, and re-layouts  44.7 us
    ppermute x8, waiting for transfers between devices, group_put(): ppermute(response[-1] if response else inp, axis_name, inbox)  40.4 us
  transfers between devices with their start and end apart: 32, of which 24 were waited for; matrix products, arithmetic and copies ran while one was open for 14% of the time, Pallas kernels for 0%

profile of v1, /device:TPU:0, one launch (start us, length us, event | category | flops | bytes accessed | tf_op | source)
XLA Modules:
  0.0 1394.8 jit_solution(15779288597856709453)
XLA Ops:
  17.4 65.6 %all-reduce.11 = (bf16[6912]{0:T(1024)(128)(2,1)S(1)}, bf16[1152]{0:T(1024)(128)(2,1)}, bf16[4608]{0:T(1024)(128)(2,1)}, bf16[1152]{0:T(1024)(128)(2,1)}) all-reduce(bf16[6912]{0:T(1024)(128)(2,1)S(1)} %dynamic-update-slice, bf16[1152]{0:T(1024)(128)(2,1)S(1)} %dynamic-update-slice.1, ...), channel_id=1, replica_groups=mesh['fsdp'=16,'tp'=2] {'fsdp'}, use_global_device_ids=true, to_apply=%add | all-reduce | flops 13824 | bytes 55296
  85.0 6.6 all-gather.10.cloned.1.call-done
  91.5 5.9 convolution_reduce_fusion
  97.5 8.3 psum.28
  109.2 19.0 %all-gather = bf16[16,72,2]{1,2,0:T(2,128)(2,1)S(1)} all-gather(bf16[1,72,2]{1,2,0:T(2,128)(2,1)S(1)} %bitcast.267), channel_id=1, replica_groups=mesh['fsdp'=16,'tp'=2] {'fsdp'}, dimensions={0}, use_global_device_ids=true | all-gather | bytes 4896 | tf_op jit(solution)/shard_map/all_gather | solution.py:120
  128.6 15.1 %all-gather.14.cloned.1.call-done = bf16[1152,3,576]{2,0,1:T(8,128)(2,1)} async-done(((bf16[72,3,576]{2,0,1:T(8,128)(2,1)}), bf16[1152,3,576]{2,0,1:T(8,128)(2,1)}) %all-gather.14.cloned.1.call-update) | async-done | bytes 3981328 | tf_op jit(solution)/shard_map/all_gather | solution.py:119
  143.7 6.6 copy.43
  150.3 30.2 %all-gather.12.cloned.1.call-done = bf16[1024,1152]{1,0:T(8,128)(2,1)} async-done(((bf16[512,1152]{1,0:T(8,128)(2,1)}), bf16[1024,1152]{1,0:T(8,128)(2,1)}) %all-gather.12.cloned.1.call-update) | async-done | bytes 2359312 | tf_op jit(solution)/shard_map/all_gather | solution.py:146
  180.4 7.3 fusion.40
  194.2 24.2 %while.27 = (s32[]{:T(128)}, bf16[2,8,512,72]{2,3,1,0:T(8,128)(2,1)}, f32[2,8,512]{2,1,0:T(8,128)}, bf16[2,8,512,72]{2,3,1,0:T(8,128)(2,1)S(1)}, bf16[8,1024,72]...) while((s32[]{:T(128)}, bf16[2,8,512,72]{2,3,1,0:T(8,128)(2,1)}, ...), condition=%wide.region_6.7_spmd, body=%wide.region_3.6_spmd.sunk | while | flops 1245704192 | bytes 64291024 | solution.py:176
  200.2 4.4 fusion.135
  212.3 4.4 fusion.135
  221.9 6.1 fusion.83
  228.4 9.2 collective-permute-done
  238.3 4.4 collective-permute-start.8
  242.7 4.9 collective-permute-done.1
  247.7 4.6 collective-permute-start.9
  252.3 4.7 collective-permute-done.2
  257.0 4.6 collective-permute-start.10
  261.7 4.7 collective-permute-done.3
  267.1 4.6 collective-permute-start.11
  276.4 4.8 collective-permute-start.12
  286.1 4.7 collective-permute-start.13
  296.8 4.6 collective-permute-start.14
  301.4 5.1 collective-permute-done.7
  334.3 5.9 gather_fusion
  340.2 7.8 all-gather.20.cloned.1.call-done
  348.0 36.9 %all-gather.18.cloned.1.call-done = bf16[1024,1152]{1,0:T(8,128)(2,1)} async-done(((bf16[512,1152]{1,0:T(8,128)(2,1)}), bf16[1024,1152]{1,0:T(8,128)(2,1)}) %all-gather.18.cloned.1.call-update) | async-done | bytes 2359312 | tf_op jit(solution)/shard_map/all_gather | solution.py:188
  384.8 11.4 fusion.84
  396.3 26.8 %all-gather.22.cloned.1.call-done = bf16[1024,1152]{1,0:T(8,128)(2,1)} async-done(((bf16[512,1152]{1,0:T(8,128)(2,1)}), bf16[1024,1152]{1,0:T(8,128)(2,1)}) %all-gather.22.cloned.1.call-update) | async-done | bytes 2359312 | tf_op jit(solution)/shard_map/all_gather | solution.py:207
  423.1 15.5 %convert_reduce_fusion = (bf16[2304]{0:T(1024)(128)(2,1)}, bf16[1024,2304]{1,0:T(8,128)(2,1)S(1)}) fusion(f32[1024,2304]{1,0:T(8,128)} %fusion.84, f32[2304]{0:T(1024)} %dynamic-slice_convert_fusion, bf16[1024,1152]{1,0:T(8,128)(2,1)} %all-gather.22.cloned.1.call-done, bf16[2304,1152]{0,1:T(8,128)(2,1)} %bitcast.254), kind=kOutput, calls=%fused_computation.51 | convolution fusion | flops 5490079744 | bytes 21837312 | tf_op jit(solution)/shard_map/dot_general | solution.py:67
  440.8 7.9 fusion.85
  449.0 13.5 convolution_convert_fusion
  463.8 45.1 %reduce-scatter.17.cloned.1.call-done = f32[512,1152]{1,0:T(8,128)} async-done(((f32[1024,1152]{1,0:T(8,128)}), f32[512,1152]{1,0:T(8,128)}) %reduce-scatter.17.cloned.1.call-update) | async-done | bytes 2359312 | tf_op jit(solution)/shard_map/reduce_scatter | solution.py:216
  513.4 32.3 %reduce-scatter.15.cloned.1.call-done = bf16[512,1152]{1,0:T(8,128)(2,1)} async-done(((bf16[1024,1152]{1,0:T(8,128)(2,1)}), bf16[512,1152]{1,0:T(8,128)(2,1)}) %reduce-scatter.15.cloned.1.call-update) | async-done | bytes 1179664 | tf_op jit(solution)/shard_map/reduce_scatter | solution.py:198
  545.7 6.1 multiply_reduce_fusion.3
  554.5 36.2 %all-gather.24.cloned.1.call-done = bf16[1024,1152]{1,0:T(8,128)(2,1)} async-done(((bf16[512,1152]{1,0:T(8,128)(2,1)}), bf16[1024,1152]{1,0:T(8,128)(2,1)}) %all-gather.24.cloned.1.call-update) | async-done | bytes 2359312 | tf_op jit(solution)/shard_map/all_gather | solution.py:225
  590.7 4.8 convolution_convert_fusion.1
  595.5 4.0 reshape.224
  603.2 117.3 %while.28 = (s32[]{:T(128)}, f32[8,1024,72]{1,2,0:T(8,128)}, f32[8,1024,72]{1,2,0:T(8,128)}, bf16[2,8,512,72]{2,3,1,0:T(8,128)(2,1)}, bf16[2,8,512,72]{2,3,1,0:T...) while((s32[]{:T(128)}, f32[8,1024,72]{1,2,0:T(8,128)}, ...), condition=%wide.region_16.17_spmd.clone, body=%wide.region_14.16_spmd.clone.sunk | while | flops 3073470464 | bytes 271434112 | solution.py:270
  604.4 8.2 fusion.145
  612.6 10.3 select_add_fusion.5
  622.9 14.5 %multiply_reduce_fusion.10 = (f32[8,512]{1,0:T(8,128)S(1)}, f32[8,512,1024]{2,1,0:T(8,128)}) fusion(f32[8,512,1024]{2,1,0:T(8,128)} %fusion.145, f32[8,512]{1,0:T(8,128)S(1)} %dynamic-slice_bitcast_fusion.3, bf16[8,1024,72]{1,2,0:T(8,128)(2,1)} %copy-done.8, bf16[2,8,512,72]{2,3,1,0:T(8,128)(2,1)} %get-tuple-element.402, s32[]{:T(128)S(6)} %copy.93), kind=kOutput, calls=%fused_computation.15.clone.1 | convolution fusion | flops 620752896 | bytes 35356676 | tf_op jit(solution)/shard_map/while/body/eval_jaxpr/hqd,hkd->hqk/dot_general | solution.py:245
  639.7 10.5 multiply_convert_fusion.8
  650.2 7.3 fusion.146
  661.5 8.2 fusion.145
  669.7 11.1 select_add_fusion.5
  680.8 14.5 %multiply_reduce_fusion.10 = (f32[8,512]{1,0:T(8,128)S(1)}, f32[8,512,1024]{2,1,0:T(8,128)}) fusion(f32[8,512,1024]{2,1,0:T(8,128)} %fusion.145, f32[8,512]{1,0:T(8,128)S(1)} %dynamic-slice_bitcast_fusion.3, bf16[8,1024,72]{1,2,0:T(8,128)(2,1)} %copy-done.8, bf16[2,8,512,72]{2,3,1,0:T(8,128)(2,1)} %get-tuple-element.402, s32[]{:T(128)S(6)} %copy.93), kind=kOutput, calls=%fused_computation.15.clone.1 | convolution fusion | flops 620752896 | bytes 35356676 | tf_op jit(solution)/shard_map/while/body/eval_jaxpr/hqd,hkd->hqk/dot_general | solution.py:245
  697.6 10.5 multiply_convert_fusion.8
  708.1 7.3 fusion.146
  715.4 5.0 select_add_fusion.4
  725.0 7.1 bitcast_convert_fusion
  732.1 5.8 fusion.86
  738.7 12.4 fusion.75
  751.1 11.3 fusion.87
  762.7 9.5 fusion.42
  781.4 8.6 all-reduce.12
  789.9 7.3 broadcast_multiply_fusion
  802.1 4.9 convolution_reduce_fusion.1
  807.6 61.9 %all-reduce.10 = (f32[6912]{0:T(1024)}, f32[2,1152]{1,0:T(2,128)}, f32[1152]{0:T(1024)}, f32[4608]{0:T(1024)}, f32[1152]{0:T(1024)}) all-reduce(bf16[6912]{0:T(1024)(128)(2,1)} %copy-done.41, bf16[2,1152]{1,0:T(2,128)(2,1)} %get-tuple-element.224, f32[1152]{0:T(1024)} %convert_reduce_fusion.2, ...), channel_id=7, replica_groups=mesh['fsdp'=16,'tp'=2] {'fsdp'}, use_global_device_ids=true, to_apply=%region_28.29.clone | all-reduce | flops 16128 | bytes 101376
  880.6 80.3 %reduce-scatter.27.cloned.1.call-done = f32[2304,72]{0,1:T(8,128)} async-done(((f32[2304,1152]{0,1:T(8,128)}), f32[2304,72]{0,1:T(8,128)}) %reduce-scatter.27.cloned.1.call-update) | async-done | bytes 663568 | tf_op jit(solution)/shard_map/reduce_scatter | solution.py:333
  960.8 124.5 %reduce-scatter.25.cloned.1.call-done = f32[72,2304]{1,0:T(8,128)} async-done(((f32[1152,2304]{1,0:T(8,128)}), f32[72,2304]{1,0:T(8,128)}) %reduce-scatter.25.cloned.1.call-update) | async-done | bytes 663568 | tf_op jit(solution)/shard_map/reduce_scatter | solution.py:331
  1085.3 111.3 %reduce-scatter.23.cloned.1.call-done = f32[72,3,576]{2,0,1:T(8,128)} async-done(((f32[1152,3,576]{2,0,1:T(8,128)}), f32[72,3,576]{2,0,1:T(8,128)}) %reduce-scatter.23.cloned.1.call-update) | async-done | bytes 497680 | tf_op jit(solution)/shard_map/reduce_scatter | solution.py:327
  1196.7 191.4 %reduce-scatter.21.cloned.1.call-done = f32[576,432]{0,1:T(8,128)} async-done(((f32[576,6912]{0,1:T(8,128)}), f32[576,432]{0,1:T(8,128)}) %reduce-scatter.21.cloned.1.call-update) | async-done | bytes 995344 | tf_op jit(solution)/shard_map/reduce_scatter | solution.py:325
  (322 shorter events, 137.1 us)
Async XLA Ops:
  7.2 77.3 %copy-start.10 = (bf16[1,512,1152]{2,1,0:T(8,128)(2,1)S(1)}, bf16[1,512,1152]{2,1,0:T(8,128)(2,1)}, u32[]{:S(2)}) copy-start(bf16[1,512,1152]{2,1,0:T(8,128)(2,1)} %param.17) | copy-start | bytes 3538948
  7.2 84.4 %all-gather.10.cloned.1.call-start = ((), (), s32[]{:S(2)}) async-start(), calls=%async_computation.9 | async-start | bytes 9400320 | tf_op jit(solution)/shard_map/all_gather | solution.py:117
  7.9 135.8 %all-gather.14.cloned.1.call-start = ((), (), s32[]{:S(2)}) async-start(), calls=%async_computation.11 | async-start | bytes 4700160 | tf_op jit(solution)/shard_map/all_gather | solution.py:119
  8.7 171.8 %all-gather.12.cloned.1.call-start = ((), (), s32[]{:S(2)}) async-start(), calls=%async_computation.10 | async-start | bytes 3538944 | tf_op jit(solution)/shard_map/all_gather | solution.py:146
  84.5 22.0 %copy-start.45 = (f32[512]{0:T(512)}, f32[512]{0:T(512)S(1)}, u32[]{:S(2)}) copy-start(f32[512]{0:T(512)S(1)} %broadcast_multiply_fusion.6) | copy-start | bytes 6148
  85.0 21.5 %copy-start.50 = (f32[512]{0:T(512)}, f32[512]{0:T(512)S(1)}, u32[]{:S(2)}) copy-start(f32[512]{0:T(512)S(1)} %add_rsqrt_fusion.1) | copy-start | bytes 6148
  97.5 11.8 copy-start.62
  108.6 113.3 %all-gather.16.cloned.1.call-start = ((), (), s32[]{:S(2)}) async-start(), calls=%async_computation.12 | async-start | bytes 1566720 | tf_op jit(solution)/shard_map/all_gather | solution.py:121
  109.2 208.7 %reduce-scatter.13.cloned.1.call-start = ((), (), s32[]{:S(2)}) async-start(), calls=%async_computation.13 | async-start | bytes 7077888 | tf_op jit(solution)/shard_map/reduce_scatter | solution.py:180
  228.0 57.3 %copy-start.61 = (bf16[1152]{0:T(1024)(128)(2,1)S(1)}, bf16[1152]{0:T(1024)(128)(2,1)}, u32[]{:S(2)}) copy-start(bf16[1152]{0:T(1024)(128)(2,1)} %get-tuple-element.220) | copy-start | bytes 6916
  228.0 120.0 %all-gather.20.cloned.1.call-start = ((), (), s32[]{:S(2)}) async-start(), calls=%async_computation.15 | async-start | bytes 5640192 | tf_op jit(solution)/shard_map/all_gather | solution.py:123
  228.1 9.5 collective-permute-start
  238.3 9.3 collective-permute-start.1
  238.3 9.4 collective-permute-start.8
  247.6 33.6 %copy-start.27 = (bf16[2304,72]{0,1:T(8,128)(2,1)}, bf16[2304,72]{0,1:T(8,128)(2,1)S(1)}, u32[]{:S(2)}) copy-start(bf16[2304,72]{0,1:T(8,128)(2,1)S(1)} %collective-permute-done.1) | copy-start | bytes 995332
  247.6 9.3 collective-permute-start.2
  247.7 28.7 %copy-start.25 = (bf16[2304,72]{0,1:T(8,128)(2,1)}, bf16[2304,72]{0,1:T(8,128)(2,1)S(1)}, u32[]{:S(2)}) copy-start(bf16[2304,72]{0,1:T(8,128)(2,1)S(1)} %collective-permute-done.8) | copy-start | bytes 995332
  247.7 9.3 collective-permute-start.9
  257.0 28.1 %copy-start.31 = (bf16[2304,72]{0,1:T(8,128)(2,1)}, bf16[2304,72]{0,1:T(8,128)(2,1)S(1)}, u32[]{:S(2)}) copy-start(bf16[2304,72]{0,1:T(8,128)(2,1)S(1)} %collective-permute-done.2) | copy-start | bytes 995332
  257.0 9.3 collective-permute-start.3
  257.0 28.1 %copy-start.29 = (bf16[2304,72]{0,1:T(8,128)(2,1)}, bf16[2304,72]{0,1:T(8,128)(2,1)S(1)}, u32[]{:S(2)}) copy-start(bf16[2304,72]{0,1:T(8,128)(2,1)S(1)} %collective-permute-done.9) | copy-start | bytes 995332
  257.0 9.3 collective-permute-start.10
  266.3 18.8 %copy-start.33 = (bf16[2304,72]{0,1:T(8,128)(2,1)}, bf16[2304,72]{0,1:T(8,128)(2,1)S(1)}, u32[]{:S(2)}) copy-start(bf16[2304,72]{0,1:T(8,128)(2,1)S(1)} %collective-permute-done.3) | copy-start | bytes 995332
  266.3 9.3 collective-permute-start.4
  267.1 9.2 collective-permute-start.11
  275.7 9.5 copy-start.35
  275.7 9.4 collective-permute-start.5
  276.4 9.8 collective-permute-start.12
  285.2 9.7 collective-permute-start.6
  285.2 99.6 %all-gather.18.cloned.1.call-start = ((), (), s32[]{:S(2)}) async-start(), calls=%async_computation.14 | async-start | bytes 3538944 | tf_op jit(solution)/shard_map/all_gather | solution.py:188
  285.3 32.6 %copy-start.44 = (f32[1152]{0:T(1024)}, f32[1152]{0:T(1024)S(1)}, u32[]{:S(2)}) copy-start(f32[1152]{0:T(1024)S(1)} %convert_element_type.164) | copy-start | bytes 13828
  285.3 27.3 %copy-start.34 = (bf16[2304,72]{0,1:T(8,128)(2,1)S(1)}, bf16[2304,72]{0,1:T(8,128)(2,1)}, u32[]{:S(2)}) copy-start(bf16[2304,72]{0,1:T(8,128)(2,1)} %copy-done.33) | copy-start | bytes 995332
  285.4 28.0 %copy-start.32 = (bf16[2304,72]{0,1:T(8,128)(2,1)S(1)}, bf16[2304,72]{0,1:T(8,128)(2,1)}, u32[]{:S(2)}) copy-start(bf16[2304,72]{0,1:T(8,128)(2,1)} %copy-done.31) | copy-start | bytes 995332
  285.4 28.8 %copy-start.28 = (bf16[2304,72]{0,1:T(8,128)(2,1)S(1)}, bf16[2304,72]{0,1:T(8,128)(2,1)}, u32[]{:S(2)}) copy-start(bf16[2304,72]{0,1:T(8,128)(2,1)} %copy-done.27) | copy-start | bytes 995332
  285.4 29.5 %copy-start.23 = (bf16[2304,72]{0,1:T(8,128)(2,1)S(1)}, bf16[2304,72]{0,1:T(8,128)(2,1)}, u32[]{:S(2)}) copy-start(bf16[2304,72]{0,1:T(8,128)(2,1)} %copy-done.22) | copy-start | bytes 995332
  286.1 10.7 collective-permute-start.13
  294.8 11.7 collective-permute-start.7
  296.8 35.7 %collective-permute-start.14 = (bf16[2304,72]{0,1:T(8,128)(2,1)}, bf16[2304,72]{0,1:T(8,128)(2,1)}, u32[]{:S(2)}, u32[]{:S(2)}) collective-permute-start(bf16[2304,72]{0,1:T(8,128)(2,1)} %collective-permute-done.13), channel_id=1, source_target_pairs={{2,0},{4,2},{6,4},{8,6},{10,8},{12,10},{14,12},{16,14},{18,16},{20... | collective-permute-start | bytes 995336 | tf_op jit(solution)/shard_map/ppermute | solution.py:36
  307.3 8.4 copy-start.21
  309.0 7.4 copy-start.26
  323.4 99.7 %all-gather.22.cloned.1.call-start = ((), (), s32[]{:S(2)}) async-start(), calls=%async_computation.17 | async-start | bytes 3538944 | tf_op jit(solution)/shard_map/all_gather | solution.py:207
  330.7 178.1 %reduce-scatter.17.cloned.1.call-start = ((), (), s32[]{:S(2)}) async-start(), calls=%async_computation.18 | async-start | bytes 7077888 | tf_op jit(solution)/shard_map/reduce_scatter | solution.py:216
  423.1 17.6 %copy-start.63 = (bf16[1152,2304]{1,0:T(8,128)(2,1)S(1)}, bf16[1152,2304]{1,0:T(8,128)(2,1)}, u32[]{:S(2)}) copy-start(bf16[1152,2304]{1,0:T(8,128)(2,1)} %all-gather.20.cloned.1.call-done) | copy-start | bytes 15925252
  448.7 97.0 %reduce-scatter.15.cloned.1.call-start = ((), (), s32[]{:S(2)}) async-start(), calls=%async_computation.16 | async-start | bytes 3538944 | tf_op jit(solution)/shard_map/reduce_scatter | solution.py:198
  462.5 128.2 %all-gather.24.cloned.1.call-start = ((), (), s32[]{:S(2)}) async-start(), calls=%async_computation.19 | async-start | bytes 3538944 | tf_op jit(solution)/shard_map/all_gather | solution.py:225
  554.5 220.9 %reduce-scatter.19.cloned.1.call-start = ((), (), s32[]{:S(2)}) async-start(), calls=%async_computation.20 | async-start | bytes 3538944 | tf_op jit(solution)/shard_map/reduce_scatter | solution.py:281
  603.6 9.0 copy-start.2
  603.6 8.9 copy-start.4
  603.6 8.9 copy-start.8
  622.8 16.9 %copy-start = (f32[8,512,1024]{2,1,0:T(8,128)S(1)}, f32[8,512,1024]{2,1,0:T(8,128)}, u32[]{:S(2)}) copy-start(f32[8,512,1024]{2,1,0:T(8,128)} %fusion.145) | copy-start | bytes 50331652 | tf_op jit(solution)/shard_map/while
  660.7 8.9 copy-start.2
  660.7 8.9 copy-start.4
  660.7 8.9 copy-start.8
  680.8 16.9 %copy-start = (f32[8,512,1024]{2,1,0:T(8,128)S(1)}, f32[8,512,1024]{2,1,0:T(8,128)}, u32[]{:S(2)}) copy-start(f32[8,512,1024]{2,1,0:T(8,128)} %fusion.145) | copy-start | bytes 50331652 | tf_op jit(solution)/shard_map/while
  708.1 7.3 copy-start.5
  724.9 37.8 %copy-start.14 = (bf16[1024,3,576]{0,2,1:T(8,128)(2,1)}, bf16[1024,3,576]{0,2,1:T(8,128)(2,1)S(1)}, u32[]{:S(2)}) copy-start(bf16[1024,3,576]{0,2,1:T(8,128)(2,1)S(1)} %maximum_convert_fusion) | copy-start | bytes 10616836
  732.1 148.5 %reduce-scatter.29.cloned.1.call-start = ((), (), s32[]{:S(2)}) async-start(), calls=%async_computation.25 | async-start | bytes 3133440
  738.0 222.9 %reduce-scatter.27.cloned.1.call-start = ((), (), s32[]{:S(2)}) async-start(), calls=%async_computation.24 | async-start | bytes 11280384 | tf_op jit(solution)/shard_map/reduce_scatter | solution.py:333
  751.1 334.3 %reduce-scatter.25.cloned.1.call-start = ((), (), s32[]{:S(2)}) async-start(), calls=%async_computation.23 | async-start | bytes 11280384 | tf_op jit(solution)/shard_map/reduce_scatter | solution.py:331
  762.4 434.2 %reduce-scatter.23.cloned.1.call-start = ((), (), s32[]{:S(2)}) async-start(), calls=%async_computation.22 | async-start | bytes 9400320 | tf_op jit(solution)/shard_map/reduce_scatter | solution.py:327
  772.2 615.8 %reduce-scatter.21.cloned.1.call-start = ((), (), s32[]{:S(2)}) async-start(), calls=%async_computation.21 | async-start | bytes 18800640 | tf_op jit(solution)/shard_map/reduce_scatter | solution.py:325
  775.1 14.8 %copy-start.58 = (f32[576]{0:T(1024)S(1)}, f32[576]{0:T(1024)}, u32[]{:S(2)}) copy-start(f32[576]{0:T(1024)} %get-tuple-element.226) | copy-start | bytes 6916
  789.9 7.3 copy-start.41
  802.1 75.3 %copy-start.13 = (f32[512,1152]{1,0:T(8,128)S(1)}, f32[512,1152]{1,0:T(8,128)}, u32[]{:S(2)}) copy-start(f32[512,1152]{1,0:T(8,128)} %copy-done.12) | copy-start | bytes 7077892
  (47 other events, 152.9 us)
Sparse Core Ops, SparseCore 0:
  10.2 81.3 all-gather.9
  93.7 49.9 all-gather.13
  145.8 34.5 all-gather.11
  182.4 39.3 all-gather.15
  228.1 58.9 reduce-scatter.12
  289.4 58.5 all-gather.19
  350.2 34.6 all-gather.17
  387.0 36.0 all-gather.21
  448.8 59.9 reduce-scatter.16
  511.0 34.7 reduce-scatter.14
  554.6 36.0 all-gather.23
  732.2 34.6 reduce-scatter.18
  771.4 65.4 reduce-scatter.28
  841.4 119.4 reduce-scatter.26
  965.3 119.9 reduce-scatter.24
  1089.9 106.6 reduce-scatter.22
  1201.8 186.1 reduce-scatter.20
